TPU v7x, 512 devices: a whole 4x4x16 slice. The times are simulated.
512 devices in a mesh: ctx: 64 (over y, z), head: 8 (over x, core).
Axes of the slice: x: 4, y: 4, z: 16, core: 2. Of those that a mesh axis runs over, the one named last changes fastest.
Arguments:
- lin_query: bfloat16 [8192, 64, 128], P('ctx', 'head'), may hold values from -6 to 6
- lin_key: bfloat16 [8192, 64, 128], P('ctx', 'head'), may hold values from -6 to 6
- lin_value: bfloat16 [8192, 64, 128], P('ctx', 'head'), may hold values from -18 to 18
- log_decay: float32 [64, 8192], P('head', 'ctx'), may hold values from -1 to 0
- norm_gain: float32 [64, 128], P('head'), may hold values from 0.5 to 1.5
- attn_query: bfloat16 [8192, 64, 128], P('ctx', 'head'), may hold values from -30 to 30
- attn_key: bfloat16 [8192, 8, 128], P('ctx', 'head'), may hold values from -16 to 16
- attn_value: bfloat16 [8192, 8, 128], P('ctx', 'head'), may hold values from -6 to 6
Outputs:
- lin_out: bfloat16 [8192, 64, 128], P('ctx', 'head')
- attn_out: bfloat16 [8192, 64, 128], P('ctx', 'head')
All inputs are finite; a program needn't handle non-finite values.
Results may differ from a plain program's by a relative error of at most 0.0055.
Values may be sent and summed in bfloat16 or wider, within the bound.
No kernel may reach another device: no remote copies, remote signals or barrier semaphores. Data moves between devices by JAX's collectives and lax.ppermute only.
A program may use at most 192 MiB of HBM per device.

v0:
```python
import jax
import jax.numpy as jnp
from jax import lax
from jax.sharding import PartitionSpec as P

QUERY_HEADS = 64
HD = 128


def carried_in(x, axis, combine, identity):
    size, mine = (lax.axis_size(axis), lax.axis_index(axis))
    everything = jax.tree.map(lambda part: lax.all_gather(part, axis), x)
    start = jax.tree.map(
        lambda part, zero: jnp.broadcast_to(jnp.asarray(zero, part.dtype), part.shape), x, identity
    )

    def hop(k, before):
        reached = k < mine
        new = combine(before, jax.tree.map(lambda part: part[k], everything))
        return jax.tree.map(lambda a, b: jnp.where(reached, a, b), new, before)

    return lax.fori_loop(0, size, hop, start)


def act_round(values):
    return jax.nn.silu(values.astype(jnp.float32)).astype(jnp.bfloat16)


def chain_state(earlier, later):
    decay_early, state_early = earlier
    decay_late, state_late = later
    return (decay_early * decay_late, decay_late[:, None, None] * state_early + state_late)


def lightning(lin_query, lin_key, lin_value, log_decay, norm_gain):
    act_query = act_round(lin_query)
    act_key = act_round(lin_key)
    act_value = act_round(lin_value)
    token_position = jnp.arange(lin_query.shape[0])
    cumulative = jnp.cumsum(log_decay, axis=1)
    causal = token_position[:, None] >= token_position[None, :]
    spread = cumulative[:, :, None] - cumulative[:, None, :]
    decay_matrix = jnp.exp(jnp.where(causal[None], spread, -1e30))
    scores = jnp.einsum("thd,shd->hts", act_query, act_key, preferred_element_type=jnp.float32)
    weights = (scores * decay_matrix).astype(jnp.bfloat16)
    inner_part = jnp.einsum("hts,shd->thd", weights, act_value, preferred_element_type=jnp.float32)
    last_sum = cumulative[:, -1]
    key_factor = jnp.exp(last_sum[None, :] - cumulative.T)
    scaled_keys = (act_key.astype(jnp.float32) * key_factor[:, :, None]).astype(jnp.bfloat16)
    local_state = jnp.einsum(
        "shd,she->hde", scaled_keys, act_value, preferred_element_type=jnp.float32
    )
    identity = (jnp.ones_like(last_sum), jnp.zeros_like(local_state))
    prior_decay, prior_state = carried_in(
        (jnp.exp(last_sum), local_state), "ctx", chain_state, identity
    )
    outer_part = jnp.einsum(
        "thd,hde->the", act_query.astype(jnp.float32), prior_state, precision=lax.Precision.HIGHEST
    )
    mixed_out = inner_part + outer_part * jnp.exp(cumulative.T)[:, :, None]
    row_squares = jnp.sum(mixed_out * mixed_out, axis=(1, 2))
    total_squares = lax.psum(row_squares, "head")
    inverse = lax.rsqrt(total_squares / (QUERY_HEADS * HD) + 1e-06)
    return (mixed_out * inverse[:, None, None] * norm_gain[None]).astype(jnp.bfloat16)


def to_groups(query_rows, kv_local):
    rows = query_rows.shape[0]
    group = query_rows.shape[1] // kv_local
    shaped = query_rows.reshape(rows, kv_local, group, query_rows.shape[2]).transpose(1, 0, 2, 3)
    return shaped.reshape(kv_local, rows * group, query_rows.shape[2])


def from_groups(grouped, rows):
    kv_local = grouped.shape[0]
    group = grouped.shape[1] // rows
    shaped = grouped.reshape(kv_local, rows, group, grouped.shape[2]).transpose(1, 0, 2, 3)
    return shaped.reshape(rows, kv_local * group, grouped.shape[2])


def attend(state_now, group_query, positions, key_piece, value_piece):
    running_max, totals, accumulated = state_now
    scores = jnp.einsum(
        "gqd,pgd->gqp", group_query, key_piece, preferred_element_type=jnp.float32
    ) * HD ** (-0.5)
    key_pos = jnp.arange(key_piece.shape[0])
    visible = positions[:, None] >= key_pos[None, :]
    masked = jnp.where(visible[None], scores, -1e30)
    newest = jnp.maximum(running_max, jnp.max(masked, axis=2))
    prob_rows = jnp.where(visible[None], jnp.exp(scores - newest[:, :, None]), 0.0)
    totals = jnp.sum(prob_rows, axis=2)
    accumulated = jnp.einsum(
        "gqp,pgd->gqd",
        prob_rows.astype(jnp.bfloat16),
        value_piece,
        preferred_element_type=jnp.float32,
    )
    return (newest, totals, accumulated)


def softmax_part(attn_query, attn_key, attn_value):
    length = attn_query.shape[0]
    kv_local = attn_key.shape[1]
    group = attn_query.shape[1] // kv_local
    ctx_index = lax.axis_index("ctx")
    own_pos = ctx_index * length + jnp.arange(length)
    query_sets = [(to_groups(attn_query, kv_local), jnp.repeat(own_pos, group), length)]

    def empty_state(group_query):
        shape_rows = group_query.shape[:2]
        return (
            jnp.full(shape_rows, -1e30, jnp.float32),
            jnp.zeros(shape_rows, jnp.float32),
            jnp.zeros(group_query.shape, jnp.float32),
        )

    initial = tuple((empty_state(query_set[0]) for query_set in query_sets))
    key_piece = lax.all_gather(attn_key, "ctx", axis=0, tiled=True)
    value_piece = lax.all_gather(attn_value, "ctx", axis=0, tiled=True)
    results = []
    for query_set, state_now in zip(query_sets, initial):
        group_query, positions, set_rows = query_set
        state_now = attend(state_now, group_query, positions, key_piece, value_piece)
        results.append(state_now)
    finals = tuple(results)
    running_max, totals, accumulated = finals[0]
    grouped = (accumulated / totals[:, :, None]).astype(jnp.bfloat16)
    result = from_groups(grouped, length)
    return result


def local(lin_query, lin_key, lin_value, log_decay, norm_gain, attn_query, attn_key, attn_value):
    lin_out = lightning(lin_query, lin_key, lin_value, log_decay, norm_gain)
    attn_out = softmax_part(attn_query, attn_key, attn_value)
    return (lin_out, attn_out)


def solution(mesh):
    return jax.shard_map(
        local,
        mesh=mesh,
        in_specs=(
            P("ctx", "head", None),
            P("ctx", "head", None),
            P("ctx", "head", None),
            P("head", "ctx"),
            P("head", None),
            P("ctx", "head", None),
            P("ctx", "head", None),
            P("ctx", "head", None),
        ),
        out_specs=(P("ctx", "head", None), P("ctx", "head", None)),
        check_vma=False,
    )
```

profile of v0, /device:TPU:1, one launch (start us, length us, event | category | flops | bytes accessed | tf_op | source)
XLA Modules:
  0.0 689.5 jit_solution(787471788955299901)
XLA Ops:
  10.0 1.4 multiply_convert_fusion.1
  12.5 1.3 dynamic-slice
  14.7 123.1 %all-reduce = f32[512]{0:T(512)S(1)} all-reduce(f32[512]{0:T(512)S(1)} %dynamic-update-slice), channel_id=2, replica_groups=mesh['ctx'=64,'head'=8] {'ctx'}, use_global_device_ids=true, to_apply=%add | all-reduce | flops 512 | bytes 4096
  139.3 9.0 %all-gather.6.cloned.1.call-done = bf16[8192,1,128]{2,0,1:T(8,128)(2,1)} async-done(((bf16[128,1,128]{2,0,1:T(8,128)(2,1)}), bf16[8192,1,128]{2,0,1:T(8,128)(2,1)}) %all-gather.6.cloned.1.call-update) | async-done | bytes 2097168 | tf_op jit(solution)/shard_map/all_gather | solution.py:118
  148.3 15.5 %select_reduce_fusion = (f32[1024]{0:T(1024)S(1)}, f32[1024,8192]{1,0:T(8,128)}) fusion(s32[1024]{0:T(1024)S(1)} %ge.35, bf16[8192,1,128]{2,0,1:T(8,128)(2,1)} %all-gather.6.cloned.1.call-done, bf16[128,8,128]{2,1,0:T(8,128)(2,1)S(1)} %copy-done), kind=kOutput, calls=%fused_computation.4 | convolution fusion | flops 2181037056 | bytes 35921920 | tf_op jit(solution)/shard_map/gqd,pgd->gqp/dot_general | solution.py:83
  163.8 15.6 %fusion.1 = f32[1024]{0:T(1024)S(1)} fusion(f32[1024,8192]{1,0:T(8,128)} %get-tuple-element.140, f32[1024]{0:T(1024)S(1)} %broadcast_maximum_fusion, s32[1024]{0:T(1024)S(1)} %ge.35), kind=kLoop, calls=%fused_computation.6 | loop fusion | flops 41942016 | bytes 33566720 | tf_op jit(solution)/shard_map/reduce_sum | solution.py:91
  179.4 108.9 %all-gather.8.cloned.1.call-done = bf16[8192,1,128]{2,0,1:T(8,128)(2,1)} async-done(((bf16[128,1,128]{2,0,1:T(8,128)(2,1)}), bf16[8192,1,128]{2,0,1:T(8,128)(2,1)}) %all-gather.8.cloned.1.call-update) | async-done | bytes 2097168 | tf_op jit(solution)/shard_map/all_gather | solution.py:119
  288.3 15.6 %fusion.21 = bf16[128,8,128]{2,1,0:T(8,128)(2,1)} fusion(bf16[8192,1,128]{2,0,1:T(8,128)(2,1)} %all-gather.8.cloned.1.call-done, f32[1024,8192]{1,0:T(8,128)} %get-tuple-element.140, f32[1024]{0:T(1024)S(1)} %broadcast_maximum_fusion, s32[1024]{0:T(1024)S(1)} %ge.35, f32[1024]{0:T(1024)S(1)} %fusion.1), kind=kOutput, calls=%fused_computation.20 | convolution fusion | flops 2189688832 | bytes 35926016 | tf_op jit(solution)/shard_map/gqp,pgd->gqd/dot_general | solution.py:92
  303.8 286.3 %all-gather.10.cloned.1.call-done = f32[512,128,128]{2,1,0:T(8,128)} async-done(((f32[8,128,128]{2,1,0:T(8,128)}), f32[512,128,128]{2,1,0:T(8,128)}) %all-gather.10.cloned.1.call-update) | async-done | bytes 33554448 | tf_op jit(solution)/shard_map/all_gather | solution.py:12
  590.1 77.7 %while.14 = (s32[]{:T(128)}, f32[8,128,128]{2,1,0:T(8,128)S(1)}, s32[]{:T(128)}, f32[64,8]{1,0:T(8,128)S(1)}, f32[64,8,128,128]{3,2,1,0:T(8,128)}, /*index=5*/s32[]{:T(128)}, s32[]{:T(128)}) while((s32[]{:T(128)}, f32[8,128,128]{2,1,0:T(8,128)S(1)}, s32[]{:T(128)}, f32[64,8]{1,0:T(8,128)S(1)}, f32[64,8,128,128]{3,2,1,0:T(8,128)}, ...), condition=%wide.region_2.3_spmd.clone, body=%wide.region_1.2_spmd.clone.sunk | while | flops 524292 | bytes 1573065 | solution.py:22
  591.4 1.2 fusion.65
  592.6 1.2 fusion.65
  593.8 1.2 fusion.65
  595.0 1.2 fusion.65
  596.2 1.2 fusion.65
  597.4 1.2 fusion.65
  598.6 1.2 fusion.65
  599.9 1.2 fusion.65
  602.3 1.2 fusion.65
  604.7 1.2 fusion.65
  605.9 1.2 fusion.65
  607.1 1.2 fusion.65
  608.4 1.2 fusion.65
  669.0 12.9 %psum.7 = f32[128]{0:T(128)S(1)} all-reduce(f32[128]{0:T(128)S(1)} %get-tuple-element.137), channel_id=1, replica_groups=mesh['ctx'=64,'head'=8] {'head'}, use_global_device_ids=true, to_apply=%region_4.5 | all-reduce | flops 128 | bytes 1024 | tf_op jit(solution)/shard_map/psum | solution.py:62
  (147 shorter events, 68.2 us)
Async XLA Ops:
  7.2 141.1 %copy-start = (bf16[128,8,128]{2,1,0:T(8,128)(2,1)S(1)}, bf16[128,8,128]{2,1,0:T(8,128)(2,1)}, u32[]{:S(2)}) copy-start(bf16[128,8,128]{2,1,0:T(8,128)(2,1)} %param.15) | copy-start | bytes 786436
  7.2 141.1 %all-gather.6.cloned.1.call-start = ((), (), s32[]{:S(2)}) async-start(), calls=%async_computation | async-start | bytes 2129920 | tf_op jit(solution)/shard_map/all_gather | solution.py:118
  7.9 280.4 %all-gather.8.cloned.1.call-start = ((), (), s32[]{:S(2)}) async-start(), calls=%async_computation.1 | async-start | bytes 2129920 | tf_op jit(solution)/shard_map/all_gather | solution.py:119
  8.7 581.5 %all-gather.10.cloned.1.call-start = ((), (), s32[]{:S(2)}) async-start(), calls=%async_computation.2 | async-start | bytes 34078720 | tf_op jit(solution)/shard_map/all_gather | solution.py:12
  163.8 519.2 %copy-start.1 = (bf16[128,8,128]{2,1,0:T(8,128)(2,1)S(1)}, bf16[128,8,128]{2,1,0:T(8,128)(2,1)}, u32[]{:S(2)}) copy-start(bf16[128,8,128]{2,1,0:T(8,128)(2,1)} %param.15) | copy-start | bytes 786436
  179.4 502.4 %copy-start.2 = (f32[8,128]{1,0:T(8,128)S(1)}, f32[8,128]{1,0:T(8,128)}, u32[]{:S(2)}) copy-start(f32[8,128]{1,0:T(8,128)} %param.14) | copy-start | bytes 12292
Sparse Core Ops, SparseCore 0:
  11.0 137.2 all-gather.5
  151.2 136.9 all-gather.7
  291.2 298.8 all-gather.9
where the time goes:
time: 693 us; the launch traced here: 689 us
  waiting for transfers between devices  406 us (59%)
  blocking collectives  136 us (20%)
  other arithmetic  94.4 us (14%)
  matrix products  33.2 us (5%)
  between operations  14.5 us (2%)
    all_gather x1, waiting for transfers between devices, carried_in(): everything = jax.tree.map(lambda part: lax.all_gather(part, axis), x)  286 us
    unnamed x1, blocking collectives  123 us
    all_gather x1, waiting for transfers between devices, softmax_part(): value_piece = lax.all_gather(attn_value, 'ctx', axis=0, tiled=True)  109 us
    select_n x64, other arithmetic, hop(): return jax.tree.map(lambda a, b: jnp.where(reached, a, b), new, before)  75.1 us
    reduce_sum x1, other arithmetic, attend(): totals = jnp.sum(prob_rows, axis=2)  15.6 us
    dot_general x1, matrix products, attend(): jnp.einsum('gqp,pgd->gqd', prob_rows.astype(jnp.bfloat16), value_piece, p...  15.6 us
    dot_general x1, matrix products, attend(): jnp.einsum('gqd,pgd->gqp', group_query, key_piece, preferred_element_type...  15.5 us
  transfers between devices with their start and end apart: 3, of which 3 were waited for; matrix products, arithmetic and copies ran while one was open for 8% of the time, Pallas kernels for 0%

commit v1 on v0

--- a/solution.py
+++ b/solution.py
@@ -116,7 +116,11 @@
 
     initial = tuple((empty_state(query_set[0]) for query_set in query_sets))
     key_piece = lax.all_gather(attn_key, "ctx", axis=0, tiled=True)
-    value_piece = lax.all_gather(attn_value, "ctx", axis=0, tiled=True)
+    peers = lax.axis_size("ctx")
+    repeats = [peers if d == 0 else 1 for d in range(attn_value.ndim)]
+    value_piece = lax.all_to_all(
+        jnp.tile(attn_value, repeats), "ctx", split_axis=0, concat_axis=0, tiled=True
+    )
     results = []
     for query_set, state_now in zip(query_sets, initial):
         group_query, positions, set_rows = query_set

time: 693 us -> 577 us (0.83)
  waiting for transfers between devices: 406 us -> 178 us
  blocking collectives: 136 us -> 211 us
  starting transfers between devices: 0.11 us -> 19.4 us
  local copies, waits for them, and re-layouts: 3.57 us -> 16.1 us
    all_gather x1 -> x0, waiting for transfers between devices: 109 us -> none  [softmax_part(): value_piece = lax.all_gather(attn_value, 'ctx', axis=0, tiled=True)]
    all_gather x1, waiting for transfers between devices: 286 us -> 177 us  [carried_in(): everything = jax.tree.map(lambda part: lax.all_gather(part, axis), x)]
    unnamed x1, blocking collectives: 123 us -> 198 us
    all_to_all x0 -> x1, starting transfers between devices: none -> 19.3 us  [softmax_part(): lax.all_to_all(jnp.tile(attn_value, repeats), 'ctx', split_axis=0, concat...]
    unnamed x10 -> x14, local copies, waits for them, and re-layouts: 2.42 us -> 13.2 us
    all_gather x1, waiting for transfers between devices: 9.04 us -> 0.02 us  [softmax_part(): key_piece = lax.all_gather(attn_key, 'ctx', axis=0, tiled=True)]
  transfers between devices with their start and end apart: 3 -> 3, of which waited for: 3 -> 1; matrix products, arithmetic and copies ran while one was open for 8% -> 12% of each run, Pallas kernels for 0% -> 0%
where the time goes in v1:
time: 577 us; the launch traced here: 574 us
  blocking collectives  211 us (37%)
  waiting for transfers between devices  178 us (31%)
  other arithmetic  98 us (17%)
  matrix products  34.4 us (6%)
  starting transfers between devices  19.4 us (3%)
  local copies, waits for them, and re-layouts  16.1 us (3%)
  between operations  14.9 us (3%)
    unnamed x1, blocking collectives  198 us
    all_gather x1, waiting for transfers between devices, carried_in(): everything = jax.tree.map(lambda part: lax.all_gather(part, axis), x)  177 us
    select_n x64, other arithmetic, hop(): return jax.tree.map(lambda a, b: jnp.where(reached, a, b), new, before)  75.2 us
    all_to_all x1, starting transfers between devices, softmax_part(): lax.all_to_all(jnp.tile(attn_value, repeats), 'ctx', split_axis=0, concat...  19.3 us
    dot_general x1, matrix products, attend(): jnp.einsum('gqp,pgd->gqd', prob_rows.astype(jnp.bfloat16), value_piece, p...  16.7 us
    reduce_sum x1, other arithmetic, attend(): totals = jnp.sum(prob_rows, axis=2)  15.6 us
    dot_general x1, matrix products, attend(): jnp.einsum('gqd,pgd->gqp', group_query, key_piece, preferred_element_type...  15.5 us
    unnamed x14, local copies, waits for them, and re-layouts  13.2 us
  transfers between devices with their start and end apart: 3, of which 1 were waited for; matrix products, arithmetic and copies ran while one was open for 12% of the time, Pallas kernels for 0%

profile of v1, /device:TPU:1, one launch (start us, length us, event | category | flops | bytes accessed | tf_op | source)
XLA Modules:
  0.0 573.5 jit_solution(8702593161325133710)
XLA Ops:
  9.3 1.9 multiply_convert_fusion.1
  12.3 1.3 tile.12
  14.1 2.9 reduce.8
  17.0 4.0 reshape.92
  21.0 19.3 %all-to-all-start = ((bf16[64,2,8192]{2,1,0:T(2,128)(2,1)}), bf16[64,2,8192]{2,1,0:T(2,128)(2,1)S(1)}, u32[]{:S(2)}, u32[]{:S(2)}) async-start(bf16[64,2,8192]{2,1,0:T(2,128)(2,1)} %reshape.92), calls=%async_computation | async-start | bytes 4194304 | tf_op jit(solution)/shard_map/all_to_all | solution.py:121
  40.3 1.3 dynamic-slice
  42.5 197.7 %all-reduce = f32[512]{0:T(512)S(1)} all-reduce(f32[512]{0:T(512)S(1)} %dynamic-update-slice), channel_id=2, replica_groups=mesh['ctx'=64,'head'=8] {'ctx'}, use_global_device_ids=true, to_apply=%add | all-reduce | flops 512 | bytes 4096
  241.6 15.5 %select_reduce_fusion = (f32[1024]{0:T(1024)S(1)}, f32[1024,8192]{1,0:T(8,128)}) fusion(s32[1024]{0:T(1024)S(1)} %ge.35, bf16[8192,1,128]{2,0,1:T(8,128)(2,1)} %all-gather.5.cloned.1.call-done, bf16[128,8,128]{2,1,0:T(8,128)(2,1)S(1)} %copy-done), kind=kOutput, calls=%fused_computation.4 | convolution fusion | flops 2181037056 | bytes 35921920 | tf_op jit(solution)/shard_map/gqd,pgd->gqp/dot_general | solution.py:83
  257.1 15.6 %fusion.1 = f32[1024]{0:T(1024)S(1)} fusion(f32[1024,8192]{1,0:T(8,128)} %get-tuple-element.142, f32[1024]{0:T(1024)S(1)} %broadcast_maximum_fusion, s32[1024]{0:T(1024)S(1)} %ge.35), kind=kLoop, calls=%fused_computation.6 | loop fusion | flops 41942016 | bytes 33566720 | tf_op jit(solution)/shard_map/reduce_sum | solution.py:91
  272.7 6.8 %reshape.93 = bf16[8192,1,128]{2,1,0:T(2,128)(2,1)} reshape(bf16[64,2,8192]{2,1,0:T(2,128)(2,1)S(1)} %all-to-all-done) | data formatting | bytes 4194304
  279.4 16.7 %fusion.22 = bf16[128,8,128]{2,1,0:T(8,128)(2,1)} fusion(bf16[8192,1,128]{2,1,0:T(2,128)(2,1)} %reshape.93, f32[1024,8192]{1,0:T(8,128)} %get-tuple-element.142, f32[1024]{0:T(1024)S(1)} %broadcast_maximum_fusion, s32[1024]{0:T(1024)S(1)} %ge.35, f32[1024]{0:T(1024)S(1)} %fusion.1), kind=kOutput, calls=%fused_computation.21 | convolution fusion | flops 2189688832 | bytes 35926016 | tf_op jit(solution)/shard_map/gqp,pgd->gqd/dot_general | solution.py:92
  296.2 177.5 %all-gather.7.cloned.1.call-done = f32[512,128,128]{2,1,0:T(8,128)} async-done(((f32[8,128,128]{2,1,0:T(8,128)}), f32[512,128,128]{2,1,0:T(8,128)}) %all-gather.7.cloned.1.call-update) | async-done | bytes 33554448 | tf_op jit(solution)/shard_map/all_gather | solution.py:12
  473.6 77.9 %while.14 = (s32[]{:T(128)}, f32[8,128,128]{2,1,0:T(8,128)S(1)}, s32[]{:T(128)}, f32[64,8]{1,0:T(8,128)S(1)}, f32[64,8,128,128]{3,2,1,0:T(8,128)}, /*index=5*/s32[]{:T(128)}, s32[]{:T(128)}) while((s32[]{:T(128)}, f32[8,128,128]{2,1,0:T(8,128)S(1)}, s32[]{:T(128)}, f32[64,8]{1,0:T(8,128)S(1)}, f32[64,8,128,128]{3,2,1,0:T(8,128)}, ...), condition=%wide.region_2.3_spmd.clone, body=%wide.region_1.2_spmd.clone.sunk | while | flops 524292 | bytes 1573073 | solution.py:22
  476.1 1.2 fusion.66
  477.3 1.2 fusion.66
  480.9 1.2 fusion.66
  482.2 1.2 fusion.66
  485.8 1.2 fusion.66
  487.0 1.2 fusion.66
  490.7 1.2 fusion.66
  491.9 1.2 fusion.66
  495.6 1.2 fusion.66
  499.2 1.2 fusion.66
  552.7 12.9 %psum.7 = f32[128]{0:T(128)S(1)} all-reduce(f32[128]{0:T(128)S(1)} %get-tuple-element.139), channel_id=1, replica_groups=mesh['ctx'=64,'head'=8] {'head'}, use_global_device_ids=true, to_apply=%region_4.5 | all-reduce | flops 128 | bytes 1024 | tf_op jit(solution)/shard_map/psum | solution.py:62
  (153 shorter events, 71.7 us)
Async XLA Ops:
  7.2 234.4 %copy-start = (bf16[128,8,128]{2,1,0:T(8,128)(2,1)S(1)}, bf16[128,8,128]{2,1,0:T(8,128)(2,1)}, u32[]{:S(2)}) copy-start(bf16[128,8,128]{2,1,0:T(8,128)(2,1)} %param.15) | copy-start | bytes 786436
  7.2 234.4 %all-gather.5.cloned.1.call-start = ((), (), s32[]{:S(2)}) async-start(), calls=%async_computation.1 | async-start | bytes 2129920 | tf_op jit(solution)/shard_map/all_gather | solution.py:118
  7.9 465.7 %all-gather.7.cloned.1.call-start = ((), (), s32[]{:S(2)}) async-start(), calls=%async_computation.2 | async-start | bytes 34078720 | tf_op jit(solution)/shard_map/all_gather | solution.py:12
  21.0 251.7 %all-to-all-start = ((bf16[64,2,8192]{2,1,0:T(2,128)(2,1)}), bf16[64,2,8192]{2,1,0:T(2,128)(2,1)S(1)}, u32[]{:S(2)}, u32[]{:S(2)}) async-start(bf16[64,2,8192]{2,1,0:T(2,128)(2,1)} %reshape.92), calls=%async_computation | async-start | bytes 4194304 | tf_op jit(solution)/shard_map/all_to_all | solution.py:121
  272.6 294.0 %copy-start.1 = (bf16[128,8,128]{2,1,0:T(8,128)(2,1)S(1)}, bf16[128,8,128]{2,1,0:T(8,128)(2,1)}, u32[]{:S(2)}) copy-start(bf16[128,8,128]{2,1,0:T(8,128)(2,1)} %param.15) | copy-start | bytes 786436
  279.4 272.7 %copy-start.2 = (bf16[128,8,128]{2,1,0:T(8,128)(2,1)S(1)}, bf16[128,8,128]{2,1,0:T(8,128)(2,1)}, u32[]{:S(2)}) copy-start(bf16[128,8,128]{2,1,0:T(8,128)(2,1)} %get-tuple-element.136) | copy-start | bytes 786436
  279.4 286.1 %copy-start.3 = (f32[8,128]{1,0:T(8,128)S(1)}, f32[8,128]{1,0:T(8,128)}, u32[]{:S(2)}) copy-start(f32[8,128]{1,0:T(8,128)} %param.14) | copy-start | bytes 12292
Sparse Core Ops, SparseCore 0:
  11.0 161.7 all-gather.4
  175.7 297.8 all-gather.6
